TPU v7x, 128 devices: a whole 4x4x4 slice. The times are simulated.
128 devices in a mesh: req: 16 (over x, z), mlp: 8 (over y, core).
Axes of the slice: x: 4, y: 4, z: 4, core: 2. Of those that a mesh axis runs over, the one named last changes fastest.
Arguments:
- patches: bfloat16 [15360, 4096], P('req'), may hold values from -6 to 6
- norm_gain: float32 [4096], replicated, may hold values from 0.25 to 1.75
- norm_bias: float32 [4096], replicated, may hold values from -3 to 3
- gate_weight: bfloat16 [4096, 8192], P(None, ('req', 'mlp')), may hold values from -0.09375 to 0.09375
- up_weight: bfloat16 [4096, 8192], P(None, ('req', 'mlp')), may hold values from -0.09375 to 0.09375
- down_weight: bfloat16 [4096, 8192], P(None, ('req', 'mlp')), may hold values from -0.0625 to 0.0625
- layer_scale: float32 [4096], replicated, may hold values from 0.25 to 2.5
- projection: bfloat16 [4, 4096, 4096], P(None, 'mlp', 'req'), may hold values from -0.046875 to 0.046875
- text_rows: bfloat16 [65536, 4096], P(('req', 'mlp')), may hold values from -6 to 6
- destination: int32 [3840], replicated, may hold values from -1 to 65535, as said below
Outputs:
- patch_out: bfloat16 [15360, 4096], P('req', 'mlp')
- streams: bfloat16 [65536, 4096], P(('req', 'mlp'))
Inputs may be any that keep to these rules, and one draw needn't show every extreme that they name: `destination`: values other than -1 are distinct positions; the positions landing in one piece of 512 consecutive positions (a stream holds 8 pieces) form one run of consecutive positions, at least one and at most 30 of them, and some piece receives exactly 30.
All inputs are finite; a program needn't handle non-finite values.
Results may differ from a plain program's by a relative error of at most 0.015.
Values may be sent and summed in bfloat16 or wider, within the bound.
No kernel may reach another device: no remote copies, remote signals or barrier semaphores. Data moves between devices by JAX's collectives and lax.ppermute only.
A program may use at most 128 MiB of HBM per device.

v0:
```python
import jax
import jax.numpy as jnp
from jax import lax
from jax.sharding import PartitionSpec as P


def layer_norm(values, norm_gain, norm_bias):
    row_mean = jnp.mean(values, axis=-1, keepdims=True)
    centred = values - row_mean
    variance = jnp.mean(centred * centred, axis=-1, keepdims=True)
    return centred * lax.rsqrt(variance + 1e-06) * norm_gain + norm_bias


def shards(
    patches,
    norm_gain,
    norm_bias,
    gate_weight,
    up_weight,
    down_weight,
    layer_scale,
    projection,
    text_rows,
    destination,
):
    req_count = lax.axis_size("req")
    mlp_count = lax.axis_size("mlp")
    req_index = lax.axis_index("req")
    mlp_index = lax.axis_index("mlp")
    rows_here, model_width = patches.shape
    feat_width = model_width // mlp_count
    inputs = patches.astype(jnp.float32)
    normed = layer_norm(inputs, norm_gain, norm_bias).astype(jnp.bfloat16)
    gate_act = jnp.dot(
        normed,
        lax.all_gather(gate_weight, "req", axis=1, tiled=True),
        preferred_element_type=jnp.float32,
    )
    up_act = jnp.dot(
        normed,
        lax.all_gather(up_weight, "req", axis=1, tiled=True),
        preferred_element_type=jnp.float32,
    )
    hidden = (jax.nn.silu(gate_act) * up_act).astype(jnp.bfloat16)
    ffn_local = lax.dot_general(
        hidden,
        lax.all_gather(down_weight, "req", axis=1, tiled=True),
        (((1,), (1,)), ((), ())),
        preferred_element_type=jnp.float32,
    )
    partial_value = lax.optimization_barrier(ffn_local.astype(jnp.bfloat16)).astype(jnp.float32)
    ffn_feats = lax.psum_scatter(
        partial_value.astype(jnp.bfloat16), "mlp", scatter_dimension=1, tiled=True
    ).astype(jnp.float32)
    scale_here = lax.dynamic_slice_in_dim(layer_scale, mlp_index * feat_width, feat_width)
    own_inputs = lax.dynamic_slice_in_dim(inputs, mlp_index * feat_width, feat_width, axis=1)
    patch_out = (own_inputs + scale_here * ffn_feats).astype(jnp.bfloat16)
    merged = patch_out.reshape(rows_here // 4, 4 * feat_width)
    weight_cols = projection.reshape(4 * feat_width, projection.shape[2])
    piece_rows = text_rows.shape[0]
    slot_count = destination.shape[0]
    bucket_count = req_count * mlp_count
    capacity = slot_count // bucket_count
    is_valid = destination >= 0
    piece_ids = jnp.where(is_valid, destination // piece_rows, -1)
    offsets = destination % piece_rows
    bucket_hit = piece_ids[:, None] == jnp.arange(bucket_count, dtype=jnp.int32)[None, :]
    first_off = jnp.min(jnp.where(bucket_hit, offsets[:, None], piece_rows), axis=0)
    counts = jnp.sum(bucket_hit.astype(jnp.int32), axis=0)
    slot_first = jnp.sum(jnp.where(bucket_hit, first_off[None, :], 0), axis=1)
    slot_rank = offsets - slot_first
    stream_ids = piece_ids // mlp_count
    piece_in = piece_ids % mlp_count
    rows_at = piece_in * (req_count * capacity) + stream_ids * capacity + slot_rank
    rows_at = jnp.where(is_valid, rows_at, bucket_count * capacity)
    sources = (
        jnp.full((bucket_count * capacity,), -1, jnp.int32)
        .at[rows_at]
        .set(jnp.arange(slot_count, dtype=jnp.int32), mode="drop")
    )
    every_row = lax.all_gather(merged, "req", axis=0, tiled=True)
    picked_rows = jnp.take(every_row, jnp.maximum(sources, 0), axis=0)
    picked_rows = jnp.where(sources[:, None] >= 0, picked_rows, jnp.zeros_like(picked_rows))
    summed = lax.psum_scatter(
        jnp.dot(picked_rows, weight_cols, preferred_element_type=jnp.float32).astype(jnp.bfloat16),
        "mlp",
        scatter_dimension=0,
        tiled=True,
    )
    arrived = lax.all_to_all(summed, "req", split_axis=0, concat_axis=1, tiled=True)
    bucket_here = req_index * mlp_count + mlp_index
    start_here = first_off[bucket_here]
    count_here = counts[bucket_here]
    positions = jnp.arange(piece_rows, dtype=jnp.int32) - start_here
    inside = (positions >= 0) & (positions < count_here)
    image_rows = jnp.take(arrived, jnp.clip(positions, 0, capacity - 1), axis=0)
    streams = jnp.where(inside[:, None], image_rows, text_rows)
    return (patch_out, streams)


def solution(mesh):
    return jax.shard_map(
        shards,
        mesh=mesh,
        in_specs=(
            P("req", None),
            P(),
            P(),
            P(None, ("req", "mlp")),
            P(None, ("req", "mlp")),
            P(None, ("req", "mlp")),
            P(),
            P(None, "mlp", "req"),
            P(("req", "mlp"), None),
            P(),
        ),
        out_specs=(P("req", "mlp"), P(("req", "mlp"), None)),
        check_vma=False,
    )
```

profile of v0, /device:TPU:0, one launch (start us, length us, event | category | flops | bytes accessed | tf_op | source)
XLA Modules:
  0.0 527.9 jit_solution(9855831558795438825)
XLA Ops:
  7.2 0.7 all-gather.5.cloned.1.call-update
  8.0 0.7 all-gather.7.cloned.1.call-update
  8.7 0.7 all-gather.9.cloned.1.call-update
  9.5 4.5 convert_reduce_fusion
  14.0 1.0 copy-done.1
  14.9 2.2 multiply_reduce_fusion
  17.1 66.4 %all-gather.5.cloned.1.call-done = bf16[4096,1024]{0,1:T(8,128)(2,1)} async-done(((bf16[4096,64]{0,1:T(8,128)(2,1)}), bf16[4096,1024]{0,1:T(8,128)(2,1)}) %all-gather.5.cloned.1.call-update) | async-done | bytes 8388624 | tf_op jit(solution)/shard_map/all_gather | solution.py:36
  83.5 14.4 %fusion.31 = f32[960,1024]{1,0:T(8,128)} fusion(bf16[4096,1024]{0,1:T(8,128)(2,1)} %all-gather.5.cloned.1.call-done, bf16[960,4096]{1,0:T(8,128)(2,1)} %param.10, f32[4096]{0:T(1024)S(1)} %copy-done.4, f32[4096]{0:T(1024)S(1)} %copy-done.5, f32[960]{0:T(1024)S(1)} %add_rsqrt_fusion, f32[960]{0:T(1024)S(1)} %broadcast_multiply_fusion), kind=kOutput, calls=%fused_computation.68 | convolution fusion | flops 8076656640 | bytes 20225536 | tf_op jit(solution)/shard_map/dot_general | solution.py:34
  97.9 58.2 %all-gather.7.cloned.1.call-done = bf16[4096,1024]{0,1:T(8,128)(2,1)} async-done(((bf16[4096,64]{0,1:T(8,128)(2,1)}), bf16[4096,1024]{0,1:T(8,128)(2,1)}) %all-gather.7.cloned.1.call-update) | async-done | bytes 8388624 | tf_op jit(solution)/shard_map/all_gather | solution.py:41
  156.1 72.6 %all-gather.9.cloned.1.call-done = bf16[4096,1024]{0,1:T(8,128)(2,1)} async-done(((bf16[4096,64]{0,1:T(8,128)(2,1)}), bf16[4096,1024]{0,1:T(8,128)(2,1)}) %all-gather.9.cloned.1.call-update) | async-done | bytes 8388624 | tf_op jit(solution)/shard_map/all_gather | solution.py:47
  228.7 25.9 %convolution_convert_fusion = bf16[960,4096]{1,0:T(8,128)(2,1)} fusion(bf16[4096,1024]{0,1:T(8,128)(2,1)} %all-gather.9.cloned.1.call-done, f32[960,1024]{1,0:T(8,128)} %fusion.31, bf16[4096,1024]{0,1:T(8,128)(2,1)} %all-gather.7.cloned.1.call-done, bf16[960,4096]{1,0:T(8,128)(2,1)} %param.10, f32[4096]{0:T(1024)S(1)} %copy-done.4, f32[4096]{0:T(1024)S(1)} %copy-done.5, ...), kind=kOutput, calls=%fused_computation.13 | convolution fusion | flops 16139550720 | bytes 36478464 | tf_op jit(solution)/shard_map/dot_general | solution.py:45
  254.7 11.3 %convert_element_type.26 = f32[960,4096]{1,0:T(8,128)} convert(bf16[960,4096]{1,0:T(8,128)(2,1)} %param.10) | non-fusion elementwise | flops 3932160 | bytes 23592960 | tf_op jit(solution)/shard_map/convert_element_type | solution.py:32
  266.0 0.8 dynamic_slice.13
  266.7 37.6 %reduce-scatter.3.cloned.1.call-done = bf16[960,512]{1,0:T(8,128)(2,1)} async-done(((bf16[960,4096]{1,0:T(8,128)(2,1)}), bf16[960,512]{1,0:T(8,128)(2,1)}) %reduce-scatter.3.cloned.1.call-update) | async-done | bytes 983056 | tf_op jit(solution)/shard_map/reduce_scatter | solution.py:52
  304.3 2.2 add_convert_fusion.1
  306.5 1.5 reshape.67
  308.1 2.5 select_reduce_fusion.1
  310.6 2.4 convert_reduce_fusion.1
  313.1 14.6 %scatter_custom_fusion = s32[3840]{0:T(1024)S(1)} fusion(s32[3840]{0:T(1024)S(1)} %compare_select_fusion, s32[3840]{0:T(1024)S(1)} %iota.16, s32[]{:T(128)} %constant.104.clone.1), kind=kCustom, calls=%fused_computation.51 | custom fusion | bytes 15364 | tf_op jit(solution)/shard_map/scatter | solution.py:79
  327.7 86.2 %all-gather.11.cloned.1.call-done = bf16[3840,2048]{1,0:T(8,128)(2,1)} async-done(((bf16[240,2048]{1,0:T(8,128)(2,1)}), bf16[3840,2048]{1,0:T(8,128)(2,1)}) %all-gather.11.cloned.1.call-update) | async-done | bytes 15728656 | tf_op jit(solution)/shard_map/all_gather | solution.py:81
  413.9 37.0 %gather_fusion = bf16[3840,2048]{1,0:T(8,128)(2,1)} fusion(bf16[3840,2048]{1,0:T(8,128)(2,1)} %all-gather.11.cloned.1.call-done, s32[4096]{0:T(1024)S(1)} %pad_clamp_fusion), kind=kCustom, calls=%fused_computation | custom fusion | bytes 31472640 | tf_op jit(solution)/shard_map/jit(_take)/gather | solution.py:82
  450.9 9.9 %fusion.7 = bf16[3840,256]{1,0:T(8,128)(2,1)} fusion(bf16[2048,256]{1,0:T(8,128)(2,1)S(1)} %bitcast.13, bf16[3840,2048]{1,0:T(8,128)(2,1)} %gather_fusion, pred[3840]{0:T(1024)(128)(4,1)S(1)} %get-tuple-element.5, pred[3840]{0:T(1024)(128)(4,1)S(1)} %get-tuple-element.4), kind=kOutput, calls=%fused_computation.14 | convolution fusion | flops 4043243520 | bytes 18750976 | tf_op jit(solution)/shard_map/dot_general | solution.py:85
  460.8 0.6 dynamic_slice.14
  461.4 0.6 dynamic_slice.15
  462.1 31.9 %reduce-scatter.5.cloned.1.call-done = bf16[480,256]{1,0:T(8,128)(2,1)} async-done(((bf16[3840,256]{1,0:T(8,128)(2,1)}), bf16[480,256]{1,0:T(8,128)(2,1)}) %reduce-scatter.5.cloned.1.call-update) | async-done | bytes 245776 | tf_op jit(solution)/shard_map/reduce_scatter | solution.py:84
  494.0 1.7 all_to_all.14
  495.7 6.9 %all-to-all-start = ((bf16[16,30,256]{2,1,0:T(8,128)(2,1)}), bf16[16,30,256]{2,1,0:T(8,128)(2,1)S(1)}, u32[]{:S(2)}, u32[]{:S(2)}) async-start(bf16[16,30,256]{2,1,0:T(8,128)(2,1)} %all_to_all.14), calls=%async_computation.2 | async-start | bytes 524288 | tf_op jit(solution)/shard_map/all_to_all | solution.py:90
  502.6 1.3 fusion.27
  503.9 0.6 compare_select_fusion.1
  504.6 6.5 %all-to-all-done = bf16[16,30,256]{2,1,0:T(8,128)(2,1)S(1)} async-done(((bf16[16,30,256]{2,1,0:T(8,128)(2,1)}), bf16[16,30,256]{2,1,0:T(8,128)(2,1)S(1)}, u32[]{:S(2)}, u32[]{:S(2)}) %all-to-all-start) | async-done | bytes 245792 | tf_op jit(solution)/shard_map/all_to_all | solution.py:90
  511.4 4.4 gather_fusion.1
  515.7 5.3 select_select_fusion
  (32 shorter events, 0.7 us)
Async XLA Ops:
  7.2 443.7 %copy-start = (bf16[4,512,256]{2,1,0:T(8,128)(2,1)S(1)}, bf16[4,512,256]{2,1,0:T(8,128)(2,1)}, u32[]{:S(2)}) copy-start(bf16[4,512,256]{2,1,0:T(8,128)(2,1)} %param.17) | copy-start | bytes 3145732
  7.2 76.3 %all-gather.5.cloned.1.call-start = ((), (), s32[]{:S(2)}) async-start(), calls=%async_computation.3 | async-start | bytes 8912896 | tf_op jit(solution)/shard_map/all_gather | solution.py:36
  7.9 148.2 %all-gather.7.cloned.1.call-start = ((), (), s32[]{:S(2)}) async-start(), calls=%async_computation.4 | async-start | bytes 8912896 | tf_op jit(solution)/shard_map/all_gather | solution.py:41
  8.7 220.1 %all-gather.9.cloned.1.call-start = ((), (), s32[]{:S(2)}) async-start(), calls=%async_computation.5 | async-start | bytes 8912896 | tf_op jit(solution)/shard_map/all_gather | solution.py:47
  9.4 294.9 %reduce-scatter.3.cloned.1.call-start = ((), (), s32[]{:S(2)}) async-start(), calls=%async_computation.6 | async-start | bytes 8847360 | tf_op jit(solution)/shard_map/reduce_scatter | solution.py:52
  9.4 5.5 %copy-start.1 = (bf16[960,4096]{1,0:T(8,128)(2,1)S(1)}, bf16[960,4096]{1,0:T(8,128)(2,1)}, u32[]{:S(2)}) copy-start(bf16[960,4096]{1,0:T(8,128)(2,1)} %param.10) | copy-start | bytes 23592964
  9.5 74.1 %copy-start.4 = (f32[4096]{0:T(1024)S(1)}, f32[4096]{0:T(1024)}, u32[]{:S(2)}) copy-start(f32[4096]{0:T(1024)} %param.12) | copy-start | bytes 49156
  9.5 74.1 %copy-start.5 = (f32[4096]{0:T(1024)S(1)}, f32[4096]{0:T(1024)}, u32[]{:S(2)}) copy-start(f32[4096]{0:T(1024)} %param.11) | copy-start | bytes 49156
  254.6 159.3 %all-gather.11.cloned.1.call-start = ((), (), s32[]{:S(2)}) async-start(), calls=%async_computation.7 | async-start | bytes 16711680 | tf_op jit(solution)/shard_map/all_gather | solution.py:81
  254.7 53.4 %copy-start.3 = (s32[3840]{0:T(1024)S(1)}, s32[3840]{0:T(1024)}, u32[]{:S(2)}) copy-start(s32[3840]{0:T(1024)} %param.19) | copy-start | bytes 46084
  306.5 144.4 %copy-start.2 = (bf16[960,512]{1,0:T(8,128)(2,1)}, bf16[960,512]{1,0:T(8,128)(2,1)S(1)}, u32[]{:S(2)}) copy-start(bf16[960,512]{1,0:T(8,128)(2,1)S(1)} %add_convert_fusion.1) | copy-start | bytes 2949124
  308.0 186.0 %reduce-scatter.5.cloned.1.call-start = ((), (), s32[]{:S(2)}) async-start(), calls=%async_computation.8 | async-start | bytes 2211840 | tf_op jit(solution)/shard_map/reduce_scatter | solution.py:84
  495.7 15.4 %all-to-all-start = ((bf16[16,30,256]{2,1,0:T(8,128)(2,1)}), bf16[16,30,256]{2,1,0:T(8,128)(2,1)S(1)}, u32[]{:S(2)}, u32[]{:S(2)}) async-start(bf16[16,30,256]{2,1,0:T(8,128)(2,1)} %all_to_all.14), calls=%async_computation.2 | async-start | bytes 524288 | tf_op jit(solution)/shard_map/all_to_all | solution.py:90
Sparse Core Ops, SparseCore 0:
  10.2 73.3 all-gather.4
  85.7 70.4 all-gather.6
  158.3 70.4 all-gather.8
  254.7 49.5 reduce-scatter.2
  308.2 105.6 all-gather.10
  460.9 33.0 reduce-scatter.4
where the time goes:
time: 528 us
  waiting for transfers between devices  362 us (69%)
  local copies, waits for them, and re-layouts  62.5 us (12%)
  matrix products  50.1 us (9%)
  other arithmetic  32.3 us (6%)
  between operations  14.3 us (3%)
  starting transfers between devices  7.14 us (1%)
    all_gather x1, waiting for transfers between devices, shards(): every_row = lax.all_gather(merged, 'req', axis=0, tiled=True)  86.2 us
    all_gather x1, waiting for transfers between devices, shards(): lax.all_gather(down_weight, 'req', axis=1, tiled=True)  72.6 us
    all_gather x1, waiting for transfers between devices, shards(): lax.all_gather(gate_weight, 'req', axis=1, tiled=True)  66.4 us
    all_gather x1, waiting for transfers between devices, shards(): lax.all_gather(up_weight, 'req', axis=1, tiled=True)  58.2 us
    reduce_scatter x1, waiting for transfers between devices, shards(): lax.psum_scatter(partial_value.astype(jnp.bfloat16), 'mlp', scatter_dimen...  37.6 us
    gather x1, local copies, waits for them, and re-layouts, shards(): picked_rows = jnp.take(every_row, jnp.maximum(sources, 0), axis=0)  37 us
    reduce_scatter x1, waiting for transfers between devices, shards(): lax.psum_scatter(jnp.dot(picked_rows, weight_cols, preferred_element_type...  31.9 us
    dot_general x1, matrix products, shards(): lax.dot_general(hidden, lax.all_gather(down_weight, 'req', axis=1, tiled=...  25.9 us
  transfers between devices with their start and end apart: 7, of which 7 were waited for; matrix products, arithmetic and copies ran while one was open for 11% of the time, Pallas kernels for 0%

commit v1 on v0

--- a/solution.py
+++ b/solution.py
@@ -78,7 +78,22 @@
         .at[rows_at]
         .set(jnp.arange(slot_count, dtype=jnp.int32), mode="drop")
     )
-    every_row = lax.all_gather(merged, "req", axis=0, tiled=True)
+    ways, here, step = (lax.axis_size("req"), lax.axis_index("req"), merged.shape[0])
+    dims = [n * ways if d == 0 else n for d, n in enumerate(merged.shape)]
+    every_row = lax.dynamic_update_slice_in_dim(
+        jnp.zeros(dims, merged.dtype), merged, here * step, axis=0
+    )
+    going_up = going_down = merged
+    for far in range(1, ways // 2 + 1):
+        going_up = lax.ppermute(going_up, "req", [(d, (d + 1) % ways) for d in range(ways)])
+        every_row = lax.dynamic_update_slice_in_dim(
+            every_row, going_up, (here - far) % ways * step, axis=0
+        )
+        if 2 * far < ways:
+            going_down = lax.ppermute(going_down, "req", [(d, (d - 1) % ways) for d in range(ways)])
+            every_row = lax.dynamic_update_slice_in_dim(
+                every_row, going_down, (here + far) % ways * step, axis=0
+            )
     picked_rows = jnp.take(every_row, jnp.maximum(sources, 0), axis=0)
     picked_rows = jnp.where(sources[:, None] >= 0, picked_rows, jnp.zeros_like(picked_rows))
     summed = lax.psum_scatter(

time: 528 us -> 621 us (1.18)
  starting transfers between devices: 7.14 us -> 46.1 us
  local copies, waits for them, and re-layouts: 62.5 us -> 96.7 us
  waiting for transfers between devices: 362 us -> 377 us
    ppermute x0 -> x15, waiting for transfers between devices: none -> 98.8 us  [the longest x8 68 us: shards(): lax.ppermute(going_up, 'req', [(d, (d + 1) % ways) for d in range(ways)])]
    all_gather x1 -> x0, waiting for transfers between devices: 86.2 us -> none  [shards(): every_row = lax.all_gather(merged, 'req', axis=0, tiled=True)]
    ppermute x0 -> x15, starting transfers between devices: none -> 38.9 us  [the longest x7 37.2 us: shards(): lax.ppermute(going_down, 'req', [(d, (d - 1) % ways) for d in range(ways)])]
    dynamic_update_slice x0 -> x16, local copies, waits for them, and re-layouts: none -> 27.6 us  [the longest x8 14.5 us: shards(): lax.dynamic_update_slice_in_dim(every_row, going_up, (here - far) % ways...]
    another operation x0 -> x1, local copies, waits for them, and re-layouts: none -> 7.5 us
  transfers between devices with their start and end apart: 7 -> 21, of which waited for: 7 -> 15; matrix products, arithmetic and copies ran while one was open for 11% -> 15% of each run, Pallas kernels for 0% -> 0%
where the time goes in v1:
time: 621 us; the launch traced here: 620 us
  waiting for transfers between devices  377 us (61%)
  local copies, waits for them, and re-layouts  96.7 us (16%)
  matrix products  50.1 us (8%)
  starting transfers between devices  46.1 us (7%)
  other arithmetic  35.3 us (6%)
  between operations  14.3 us (2%)
    all_gather x1, waiting for transfers between devices, shards(): lax.all_gather(down_weight, 'req', axis=1, tiled=True)  72.6 us
    ppermute x8, waiting for transfers between devices, shards(): lax.ppermute(going_up, 'req', [(d, (d + 1) % ways) for d in range(ways)])  68 us
    all_gather x1, waiting for transfers between devices, shards(): lax.all_gather(gate_weight, 'req', axis=1, tiled=True)  64.3 us
    all_gather x1, waiting for transfers between devices, shards(): lax.all_gather(up_weight, 'req', axis=1, tiled=True)  58.2 us
    reduce_scatter x1, waiting for transfers between devices, shards(): lax.psum_scatter(partial_value.astype(jnp.bfloat16), 'mlp', scatter_dimen...  37.6 us
    reduce_scatter x1, waiting for transfers between devices, shards(): lax.psum_scatter(jnp.dot(picked_rows, weight_cols, preferred_element_type...  37.4 us
    ppermute x7, starting transfers between devices, shards(): lax.ppermute(going_down, 'req', [(d, (d - 1) % ways) for d in range(ways)])  37.2 us
    gather x1, local copies, waits for them, and re-layouts, shards(): picked_rows = jnp.take(every_row, jnp.maximum(sources, 0), axis=0)  37 us
  transfers between devices with their start and end apart: 21, of which 15 were waited for; matrix products, arithmetic and copies ran while one was open for 15% of the time, Pallas kernels for 0%

profile of v1, /device:TPU:0, one launch (start us, length us, event | category | flops | bytes accessed | tf_op | source)
XLA Modules:
  0.0 619.8 jit_solution(3724162003459512692)
XLA Ops:
  9.5 4.3 convert_reduce_fusion
  13.8 5.4 multiply_reduce_fusion
  19.2 64.3 %all-gather.4.cloned.1.call-done = bf16[4096,1024]{0,1:T(8,128)(2,1)} async-done(((bf16[4096,64]{0,1:T(8,128)(2,1)}), bf16[4096,1024]{0,1:T(8,128)(2,1)}) %all-gather.4.cloned.1.call-update) | async-done | bytes 8388624 | tf_op jit(solution)/shard_map/all_gather | solution.py:36
  83.5 14.4 %fusion.31 = f32[960,1024]{1,0:T(8,128)} fusion(bf16[4096,1024]{0,1:T(8,128)(2,1)} %all-gather.4.cloned.1.call-done, bf16[960,4096]{1,0:T(8,128)(2,1)} %param.10, f32[4096]{0:T(1024)S(1)} %copy-done.6, f32[4096]{0:T(1024)S(1)} %copy-done.7, f32[960]{0:T(1024)S(1)} %add_rsqrt_fusion, f32[960]{0:T(1024)S(1)} %broadcast_multiply_fusion), kind=kOutput, calls=%fused_computation.84 | convolution fusion | flops 8076656640 | bytes 20225536 | tf_op jit(solution)/shard_map/dot_general | solution.py:34
  97.9 58.2 %all-gather.6.cloned.1.call-done = bf16[4096,1024]{0,1:T(8,128)(2,1)} async-done(((bf16[4096,64]{0,1:T(8,128)(2,1)}), bf16[4096,1024]{0,1:T(8,128)(2,1)}) %all-gather.6.cloned.1.call-update) | async-done | bytes 8388624 | tf_op jit(solution)/shard_map/all_gather | solution.py:41
  156.1 72.6 %all-gather.8.cloned.1.call-done = bf16[4096,1024]{0,1:T(8,128)(2,1)} async-done(((bf16[4096,64]{0,1:T(8,128)(2,1)}), bf16[4096,1024]{0,1:T(8,128)(2,1)}) %all-gather.8.cloned.1.call-update) | async-done | bytes 8388624 | tf_op jit(solution)/shard_map/all_gather | solution.py:47
  228.8 25.9 %convolution_convert_fusion = bf16[960,4096]{1,0:T(8,128)(2,1)} fusion(bf16[4096,1024]{0,1:T(8,128)(2,1)} %all-gather.8.cloned.1.call-done, f32[960,1024]{1,0:T(8,128)} %fusion.31, bf16[4096,1024]{0,1:T(8,128)(2,1)} %all-gather.6.cloned.1.call-done, bf16[960,4096]{1,0:T(8,128)(2,1)} %param.10, f32[4096]{0:T(1024)S(1)} %copy-done.6, f32[4096]{0:T(1024)S(1)} %copy-done.7, ...), kind=kOutput, calls=%fused_computation.13 | convolution fusion | flops 16139550720 | bytes 36478464 | tf_op jit(solution)/shard_map/dot_general | solution.py:45
  254.7 11.3 %convert_element_type.26 = f32[960,4096]{1,0:T(8,128)} convert(bf16[960,4096]{1,0:T(8,128)(2,1)} %param.10) | non-fusion elementwise | flops 3932160 | bytes 23592960 | tf_op jit(solution)/shard_map/convert_element_type | solution.py:32
  266.8 37.6 %reduce-scatter.3.cloned.1.call-done = bf16[960,512]{1,0:T(8,128)(2,1)} async-done(((bf16[960,4096]{1,0:T(8,128)(2,1)}), bf16[960,512]{1,0:T(8,128)(2,1)}) %reduce-scatter.3.cloned.1.call-update) | async-done | bytes 983056 | tf_op jit(solution)/shard_map/reduce_scatter | solution.py:52
  312.5 20.9 %collective-permute-done = bf16[240,2048]{1,0:T(8,128)(2,1)S(1)} collective-permute-done((bf16[240,2048]{1,0:T(8,128)(2,1)S(1)}, bf16[240,2048]{1,0:T(8,128)(2,1)S(1)}, u32[]{:S(2)}, u32[]{:S(2)}) %collective-permute-start) | collective-permute-done | bytes 983072 | tf_op jit(solution)/shard_map/ppermute | solution.py:88
  333.5 5.3 collective-permute-start.3
  338.8 20.0 %collective-permute-done.2 = bf16[240,2048]{1,0:T(8,128)(2,1)S(1)} collective-permute-done((bf16[240,2048]{1,0:T(8,128)(2,1)S(1)}, bf16[240,2048]{1,0:T(8,128)(2,1)S(1)}, u32[]{:S(2)}, u32[]{:S(2)}) %collective-permute-start.2) | collective-permute-done | bytes 983072 | tf_op jit(solution)/shard_map/ppermute | solution.py:88
  359.8 5.3 collective-permute-start.5
  365.1 19.2 %collective-permute-done.4 = bf16[240,2048]{1,0:T(8,128)(2,1)} collective-permute-done((bf16[240,2048]{1,0:T(8,128)(2,1)S(1)}, bf16[240,2048]{1,0:T(8,128)(2,1)}, u32[]{:S(2)}, u32[]{:S(2)}) %collective-permute-start.4) | collective-permute-done | bytes 983072 | tf_op jit(solution)/shard_map/ppermute | solution.py:88
  389.1 14.6 %scatter_custom_fusion = s32[3840]{0:T(1024)S(1)} fusion(s32[3840]{0:T(1024)S(1)} %compare_select_fusion, s32[3840]{0:T(1024)S(1)} %iota.16, s32[]{:T(128)} %constant.186.clone.1), kind=kCustom, calls=%fused_computation.51 | custom fusion | bytes 15364 | tf_op jit(solution)/shard_map/scatter | solution.py:79
  403.7 5.4 collective-permute-start.7
  409.5 7.5 %broadcast.140 = bf16[3840,2048]{1,0:T(8,128)(2,1)} broadcast(bf16[]{:T(256)} %constant.199.clone.1), dimensions={} | broadcast | bytes 15728642 | tf_op jit(solution)/shard_map/broadcast.7
  420.3 6.5 %collective-permute-done.7 = bf16[240,2048]{1,0:T(8,128)(2,1)} collective-permute-done((bf16[240,2048]{1,0:T(8,128)(2,1)}, bf16[240,2048]{1,0:T(8,128)(2,1)}, u32[]{:S(2)}, u32[]{:S(2)}) %collective-permute-start.7) | collective-permute-done | bytes 983072 | tf_op jit(solution)/shard_map/ppermute | solution.py:93
  426.8 5.8 collective-permute-start.9
  441.7 7.7 %collective-permute-done.9 = bf16[240,2048]{1,0:T(8,128)(2,1)S(1)} collective-permute-done((bf16[240,2048]{1,0:T(8,128)(2,1)}, bf16[240,2048]{1,0:T(8,128)(2,1)S(1)}, u32[]{:S(2)}, u32[]{:S(2)}) %collective-permute-start.9) | collective-permute-done | bytes 983072 | tf_op jit(solution)/shard_map/ppermute | solution.py:93
  449.4 5.7 collective-permute-start.11
  464.2 7.1 %collective-permute-done.11 = bf16[240,2048]{1,0:T(8,128)(2,1)S(1)} collective-permute-done((bf16[240,2048]{1,0:T(8,128)(2,1)S(1)}, bf16[240,2048]{1,0:T(8,128)(2,1)S(1)}, u32[]{:S(2)}, u32[]{:S(2)}) %collective-permute-start.11) | collective-permute-done | bytes 983072 | tf_op jit(solution)/shard_map/ppermute | solution.py:93
  471.2 5.8 collective-permute-start.13
  482.4 9.4 %collective-permute-done.13 = bf16[240,2048]{1,0:T(8,128)(2,1)S(1)} collective-permute-done((bf16[240,2048]{1,0:T(8,128)(2,1)S(1)}, bf16[240,2048]{1,0:T(8,128)(2,1)S(1)}, u32[]{:S(2)}, u32[]{:S(2)}) %collective-permute-start.13) | collective-permute-done | bytes 983072 | tf_op jit(solution)/shard_map/ppermute | solution.py:93
  492.8 6.8 %collective-permute-done.14 = bf16[240,2048]{1,0:T(8,128)(2,1)S(1)} collective-permute-done((bf16[240,2048]{1,0:T(8,128)(2,1)S(1)}, bf16[240,2048]{1,0:T(8,128)(2,1)S(1)}, u32[]{:S(2)}, u32[]{:S(2)}) %collective-permute-start.14) | collective-permute-done | bytes 983072 | tf_op jit(solution)/shard_map/ppermute | solution.py:88
  500.6 37.0 %gather_fusion = bf16[3840,2048]{1,0:T(8,128)(2,1)} fusion(bf16[3840,2048]{1,0:T(8,128)(2,1)} %constant_dynamic-update-slice_fusion, s32[4096]{0:T(1024)S(1)} %pad_clamp_fusion), kind=kCustom, calls=%fused_computation | custom fusion | bytes 31472640 | tf_op jit(solution)/shard_map/jit(_take)/gather | solution.py:97
  537.6 9.9 %fusion.7 = bf16[3840,256]{1,0:T(8,128)(2,1)} fusion(bf16[2048,256]{1,0:T(8,128)(2,1)S(1)} %bitcast.12, bf16[3840,2048]{1,0:T(8,128)(2,1)} %gather_fusion, pred[3840]{0:T(1024)(128)(4,1)S(1)} %get-tuple-element.5, pred[3840]{0:T(1024)(128)(4,1)S(1)} %get-tuple-element.4), kind=kOutput, calls=%fused_computation.14 | convolution fusion | flops 4043243520 | bytes 18750976 | tf_op jit(solution)/shard_map/dot_general | solution.py:100
  548.8 37.4 %reduce-scatter.5.cloned.1.call-done = bf16[480,256]{1,0:T(8,128)(2,1)} async-done(((bf16[3840,256]{1,0:T(8,128)(2,1)}), bf16[480,256]{1,0:T(8,128)(2,1)}) %reduce-scatter.5.cloned.1.call-update) | async-done | bytes 245776 | tf_op jit(solution)/shard_map/reduce_scatter | solution.py:99
  588.0 6.9 %all-to-all-start = ((bf16[16,30,256]{2,1,0:T(8,128)(2,1)}), bf16[16,30,256]{2,1,0:T(8,128)(2,1)S(1)}, u32[]{:S(2)}, u32[]{:S(2)}) async-start(bf16[16,30,256]{2,1,0:T(8,128)(2,1)} %all_to_all.14), calls=%async_computation.2 | async-start | bytes 524288 | tf_op jit(solution)/shard_map/all_to_all | solution.py:105
  597.0 6.4 %all-to-all-done = bf16[16,30,256]{2,1,0:T(8,128)(2,1)S(1)} async-done(((bf16[16,30,256]{2,1,0:T(8,128)(2,1)}), bf16[16,30,256]{2,1,0:T(8,128)(2,1)S(1)}, u32[]{:S(2)}, u32[]{:S(2)}) %all-to-all-start) | async-done | bytes 245792 | tf_op jit(solution)/shard_map/all_to_all | solution.py:105
  603.7 4.4 gather_fusion.1
  608.0 5.3 select_select_fusion
  (80 shorter events, 51.2 us)
Async XLA Ops:
  7.2 530.4 %copy-start = (bf16[4,512,256]{2,1,0:T(8,128)(2,1)S(1)}, bf16[4,512,256]{2,1,0:T(8,128)(2,1)}, u32[]{:S(2)}) copy-start(bf16[4,512,256]{2,1,0:T(8,128)(2,1)} %param.17) | copy-start | bytes 3145732
  7.2 76.4 %copy-start.7 = (f32[4096]{0:T(1024)S(1)}, f32[4096]{0:T(1024)}, u32[]{:S(2)}) copy-start(f32[4096]{0:T(1024)} %param.11) | copy-start | bytes 49156
  7.2 76.3 %copy-start.6 = (f32[4096]{0:T(1024)S(1)}, f32[4096]{0:T(1024)}, u32[]{:S(2)}) copy-start(f32[4096]{0:T(1024)} %param.12) | copy-start | bytes 49156
  7.2 76.3 %all-gather.4.cloned.1.call-start = ((), (), s32[]{:S(2)}) async-start(), calls=%async_computation.3 | async-start | bytes 8912896 | tf_op jit(solution)/shard_map/all_gather | solution.py:36
  7.9 148.2 %all-gather.6.cloned.1.call-start = ((), (), s32[]{:S(2)}) async-start(), calls=%async_computation.4 | async-start | bytes 8912896 | tf_op jit(solution)/shard_map/all_gather | solution.py:41
  8.7 220.1 %all-gather.8.cloned.1.call-start = ((), (), s32[]{:S(2)}) async-start(), calls=%async_computation.5 | async-start | bytes 8912896 | tf_op jit(solution)/shard_map/all_gather | solution.py:47
  9.4 294.9 %reduce-scatter.3.cloned.1.call-start = ((), (), s32[]{:S(2)}) async-start(), calls=%async_computation.6 | async-start | bytes 8847360 | tf_op jit(solution)/shard_map/reduce_scatter | solution.py:52
  254.6 129.7 %copy-start.5 = (s32[3840]{0:T(1024)S(1)}, s32[3840]{0:T(1024)}, u32[]{:S(2)}) copy-start(s32[3840]{0:T(1024)} %param.19) | copy-start | bytes 46084
  254.6 331.6 %reduce-scatter.5.cloned.1.call-start = ((), (), s32[]{:S(2)}) async-start(), calls=%async_computation.7 | async-start | bytes 2211840 | tf_op jit(solution)/shard_map/reduce_scatter | solution.py:99
  306.5 150.9 %copy-start.1 = (bf16[960,512]{1,0:T(8,128)(2,1)}, bf16[960,512]{1,0:T(8,128)(2,1)S(1)}, u32[]{:S(2)}) copy-start(bf16[960,512]{1,0:T(8,128)(2,1)S(1)} %add_convert_fusion.1) | copy-start | bytes 2949124
  307.1 26.3 %collective-permute-start = (bf16[240,2048]{1,0:T(8,128)(2,1)S(1)}, bf16[240,2048]{1,0:T(8,128)(2,1)S(1)}, u32[]{:S(2)}, u32[]{:S(2)}) collective-permute-start(bf16[240,2048]{1,0:T(8,128)(2,1)S(1)} %reshape.67), channel_id=1, source_target_pairs={{0,8},{8,16},{16,24},{24,32},{32,40},{40,48},{48,56},{56,64},{64,7... | collective-permute-start | bytes 2949128 | tf_op jit(solution)/shard_map/ppermute | solution.py:88
  308.7 24.7 %collective-permute-start.1 = (bf16[240,2048]{1,0:T(8,128)(2,1)S(1)}, bf16[240,2048]{1,0:T(8,128)(2,1)S(1)}, u32[]{:S(2)}, u32[]{:S(2)}) collective-permute-start(bf16[240,2048]{1,0:T(8,128)(2,1)S(1)} %reshape.67), channel_id=1, source_target_pairs={{0,120},{8,0},{16,8},{24,16},{32,24},{40,32},{48,40},{56,48},{64,5... | collective-permute-start | bytes 2949128 | tf_op jit(solution)/shard_map/ppermute | solution.py:93
  333.4 50.8 %copy-start.4 = (bf16[240,2048]{1,0:T(8,128)(2,1)}, bf16[240,2048]{1,0:T(8,128)(2,1)S(1)}, u32[]{:S(2)}) copy-start(bf16[240,2048]{1,0:T(8,128)(2,1)S(1)} %collective-permute-done) | copy-start | bytes 2949124
  333.4 25.3 %collective-permute-start.2 = (bf16[240,2048]{1,0:T(8,128)(2,1)S(1)}, bf16[240,2048]{1,0:T(8,128)(2,1)S(1)}, u32[]{:S(2)}, u32[]{:S(2)}) collective-permute-start(bf16[240,2048]{1,0:T(8,128)(2,1)S(1)} %collective-permute-done), channel_id=1, source_target_pairs={{0,8},{8,16},{16,24},{24,32},{32,40},{40,48},{48,56},{56,64},{64,7... | collective-permute-start | bytes 2949128 | tf_op jit(solution)/shard_map/ppermute | solution.py:88
  333.4 50.8 %copy-start.3 = (bf16[240,2048]{1,0:T(8,128)(2,1)}, bf16[240,2048]{1,0:T(8,128)(2,1)S(1)}, u32[]{:S(2)}) copy-start(bf16[240,2048]{1,0:T(8,128)(2,1)S(1)} %collective-permute-done.1) | copy-start | bytes 2949124
  333.5 26.3 %collective-permute-start.3 = (bf16[240,2048]{1,0:T(8,128)(2,1)S(1)}, bf16[240,2048]{1,0:T(8,128)(2,1)}, u32[]{:S(2)}, u32[]{:S(2)}) collective-permute-start(bf16[240,2048]{1,0:T(8,128)(2,1)S(1)} %collective-permute-done.1), channel_id=1, source_target_pairs={{0,120},{8,0},{16,8},{24,16},{32,24},{40,32},{48,40},{56,48},{64,5... | collective-permute-start | bytes 2949128 | tf_op jit(solution)/shard_map/ppermute | solution.py:93
  358.8 1.0 copy-start.2
  359.8 24.5 %collective-permute-start.4 = (bf16[240,2048]{1,0:T(8,128)(2,1)S(1)}, bf16[240,2048]{1,0:T(8,128)(2,1)}, u32[]{:S(2)}, u32[]{:S(2)}) collective-permute-start(bf16[240,2048]{1,0:T(8,128)(2,1)S(1)} %collective-permute-done.2), channel_id=1, source_target_pairs={{0,8},{8,16},{16,24},{24,32},{32,40},{40,48},{48,56},{56,64},{64,7... | collective-permute-start | bytes 2949128 | tf_op jit(solution)/shard_map/ppermute | solution.py:88
  359.8 43.9 %collective-permute-start.5 = (bf16[240,2048]{1,0:T(8,128)(2,1)}, bf16[240,2048]{1,0:T(8,128)(2,1)}, u32[]{:S(2)}, u32[]{:S(2)}) collective-permute-start(bf16[240,2048]{1,0:T(8,128)(2,1)} %collective-permute-done.3), channel_id=1, source_target_pairs={{0,120},{8,0},{16,8},{24,16},{32,24},{40,32},{48,40},{56,48},{64,5... | collective-permute-start | bytes 2949128 | tf_op jit(solution)/shard_map/ppermute | solution.py:93
  384.3 24.8 %collective-permute-start.6 = (bf16[240,2048]{1,0:T(8,128)(2,1)}, bf16[240,2048]{1,0:T(8,128)(2,1)}, u32[]{:S(2)}, u32[]{:S(2)}) collective-permute-start(bf16[240,2048]{1,0:T(8,128)(2,1)} %collective-permute-done.4), channel_id=1, source_target_pairs={{0,8},{8,16},{16,24},{24,32},{32,40},{40,48},{48,56},{56,64},{64,7... | collective-permute-start | bytes 2949128 | tf_op jit(solution)/shard_map/ppermute | solution.py:88
  403.7 23.1 %collective-permute-start.7 = (bf16[240,2048]{1,0:T(8,128)(2,1)}, bf16[240,2048]{1,0:T(8,128)(2,1)}, u32[]{:S(2)}, u32[]{:S(2)}) collective-permute-start(bf16[240,2048]{1,0:T(8,128)(2,1)} %collective-permute-done.5), channel_id=1, source_target_pairs={{0,120},{8,0},{16,8},{24,16},{32,24},{40,32},{48,40},{56,48},{64,5... | collective-permute-start | bytes 2949128 | tf_op jit(solution)/shard_map/ppermute | solution.py:93
  409.1 25.8 %collective-permute-start.8 = (bf16[240,2048]{1,0:T(8,128)(2,1)}, bf16[240,2048]{1,0:T(8,128)(2,1)}, u32[]{:S(2)}, u32[]{:S(2)}) collective-permute-start(bf16[240,2048]{1,0:T(8,128)(2,1)} %collective-permute-done.6), channel_id=1, source_target_pairs={{0,8},{8,16},{16,24},{24,32},{32,40},{40,48},{48,56},{56,64},{64,7... | collective-permute-start | bytes 2949128 | tf_op jit(solution)/shard_map/ppermute | solution.py:88
  426.8 22.6 %collective-permute-start.9 = (bf16[240,2048]{1,0:T(8,128)(2,1)}, bf16[240,2048]{1,0:T(8,128)(2,1)S(1)}, u32[]{:S(2)}, u32[]{:S(2)}) collective-permute-start(bf16[240,2048]{1,0:T(8,128)(2,1)} %collective-permute-done.7), channel_id=1, source_target_pairs={{0,120},{8,0},{16,8},{24,16},{32,24},{40,32},{48,40},{56,48},{64,5... | collective-permute-start | bytes 2949128 | tf_op jit(solution)/shard_map/ppermute | solution.py:93
  434.9 22.5 %collective-permute-start.10 = (bf16[240,2048]{1,0:T(8,128)(2,1)}, bf16[240,2048]{1,0:T(8,128)(2,1)S(1)}, u32[]{:S(2)}, u32[]{:S(2)}) collective-permute-start(bf16[240,2048]{1,0:T(8,128)(2,1)} %collective-permute-done.8), channel_id=1, source_target_pairs={{0,8},{8,16},{16,24},{24,32},{32,40},{40,48},{48,56},{56,64},{64,7... | collective-permute-start | bytes 2949128 | tf_op jit(solution)/shard_map/ppermute | solution.py:88
  449.4 21.8 %collective-permute-start.11 = (bf16[240,2048]{1,0:T(8,128)(2,1)S(1)}, bf16[240,2048]{1,0:T(8,128)(2,1)S(1)}, u32[]{:S(2)}, u32[]{:S(2)}) collective-permute-start(bf16[240,2048]{1,0:T(8,128)(2,1)S(1)} %collective-permute-done.9), channel_id=1, source_target_pairs={{0,120},{8,0},{16,8},{24,16},{32,24},{40,32},{48,40},{56,48},{64,5... | collective-permute-start | bytes 2949128 | tf_op jit(solution)/shard_map/ppermute | solution.py:93
  457.4 21.9 %collective-permute-start.12 = (bf16[240,2048]{1,0:T(8,128)(2,1)S(1)}, bf16[240,2048]{1,0:T(8,128)(2,1)S(1)}, u32[]{:S(2)}, u32[]{:S(2)}) collective-permute-start(bf16[240,2048]{1,0:T(8,128)(2,1)S(1)} %collective-permute-done.10), channel_id=1, source_target_pairs={{0,8},{8,16},{16,24},{24,32},{32,40},{40,48},{48,56},{56,64},{64,7... | collective-permute-start | bytes 2949128 | tf_op jit(solution)/shard_map/ppermute | solution.py:88
  471.2 20.5 %collective-permute-start.13 = (bf16[240,2048]{1,0:T(8,128)(2,1)S(1)}, bf16[240,2048]{1,0:T(8,128)(2,1)S(1)}, u32[]{:S(2)}, u32[]{:S(2)}) collective-permute-start(bf16[240,2048]{1,0:T(8,128)(2,1)S(1)} %collective-permute-done.11), channel_id=1, source_target_pairs={{0,120},{8,0},{16,8},{24,16},{32,24},{40,32},{48,40},{56,48},{64,5... | collective-permute-start | bytes 2949128 | tf_op jit(solution)/shard_map/ppermute | solution.py:93
  479.3 20.2 %collective-permute-start.14 = (bf16[240,2048]{1,0:T(8,128)(2,1)S(1)}, bf16[240,2048]{1,0:T(8,128)(2,1)S(1)}, u32[]{:S(2)}, u32[]{:S(2)}) collective-permute-start(bf16[240,2048]{1,0:T(8,128)(2,1)S(1)} %collective-permute-done.12), channel_id=1, source_target_pairs={{0,8},{8,16},{16,24},{24,32},{32,40},{40,48},{48,56},{56,64},{64,7... | collective-permute-start | bytes 2949128 | tf_op jit(solution)/shard_map/ppermute | solution.py:88
  588.0 15.4 %all-to-all-start = ((bf16[16,30,256]{2,1,0:T(8,128)(2,1)}), bf16[16,30,256]{2,1,0:T(8,128)(2,1)S(1)}, u32[]{:S(2)}, u32[]{:S(2)}) async-start(bf16[16,30,256]{2,1,0:T(8,128)(2,1)} %all_to_all.14), calls=%async_computation.2 | async-start | bytes 524288 | tf_op jit(solution)/shard_map/all_to_all | solution.py:105
Sparse Core Ops, SparseCore 0:
  10.2 73.3 all-gather.3
  85.7 70.4 all-gather.5
  158.3 70.4 all-gather.7
  254.8 49.5 reduce-scatter.2
  547.7 38.5 reduce-scatter.4
